TPU v7x, 256 devices: a whole 4x4x8 slice. The times are simulated.
256 devices in a mesh: seq: 64 (over y, z, core), section: 4 (over x).
Axes of the slice: x: 4, y: 4, z: 8, core: 2. Of those that a mesh axis runs over, the one named last changes fastest.
Arguments:
- acts: bfloat16 [16384, 1408], P('seq'), may hold values from -16 to 16
- pre_act: bfloat16 [16384, 1536], P('seq', 'section'), may hold values from -6 to 6
- emb_grad: bfloat16 [8192, 1536], P('seq', 'section'), may hold values from -6 to 6
- filters: bfloat16 [7040, 1536], P('seq', 'section'), may hold values from -0.0625 to 0.0625
Outputs:
- input_grad: bfloat16 [16384, 1408], P('seq', 'section')
- filter_grad: float32 [7040, 1536], P('seq', 'section')
All inputs are finite; a program needn't handle non-finite values.
Results may differ from a plain program's by a relative error of at most 0.0049.
Values may be sent and summed in bfloat16 or wider, within the bound.
A program may use at most 128 MiB of HBM per device.

v0:
```python
import math
import jax
import jax.numpy as jnp
from jax import lax
from jax.sharding import PartitionSpec as P

KERNEL = 5
SEQS = 1


def with_halo(shard, sides, width):
    for axis, dim in sides:
        size, length = (lax.axis_size(axis), shard.shape[dim])
        up = [(i, (i + 1) % size) for i in range(size - 1)]
        down = [(j, i) for i, j in up]
        last = lax.slice_in_dim(shard, length - width, length, axis=dim)
        first = lax.slice_in_dim(shard, 0, width, axis=dim)
        before = lax.ppermute(last, axis, up)
        after = lax.ppermute(first, axis, down)
        shard = jnp.concatenate([before, shard, after], axis=dim)
    return shard


def gelu_slope(value):
    cumul = 0.5 * (1.0 + lax.erf(value * 0.7071067811865476))
    dens = jnp.exp(-0.5 * value * value) * 0.3989422804014327
    return cumul + value * dens


def shards(acts, pre_act, emb_grad, filters):
    rows = acts.shape[0]
    c_in = acts.shape[1]
    upward = jnp.repeat(emb_grad.astype(jnp.float32), 2, axis=0) * 0.5
    zvalue = pre_act.astype(jnp.float32)
    dz_grad = (upward * gelu_slope(zvalue)).astype(jnp.bfloat16)
    total_rows = rows * lax.axis_size("seq")
    length = total_rows // SEQS
    first = lax.axis_index("seq") * rows
    positions = first - 2 + jnp.arange(rows + 4, dtype=jnp.int32)
    inside = (jnp.floor_divide(positions, length) == first // length).astype(jnp.bfloat16)[:, None]
    scale_value = 1.0 / math.sqrt(total_rows)
    grad_rim = with_halo(dz_grad, (("seq", 0),), 2) * inside
    whole_term = (
        jnp.concatenate(
            [
                jnp.einsum(
                    "rc,ro->co",
                    acts,
                    grad_rim[4 - k : 4 - k + rows],
                    preferred_element_type=jnp.float32,
                )
                for k in range(KERNEL)
            ],
            axis=0,
        )
        * scale_value
    )
    piece = lax.all_gather(filters, "seq", axis=0, tiled=True)
    width = piece.shape[0]
    product = jnp.einsum("ro,no->rn", grad_rim, piece, preferred_element_type=jnp.float32)
    tap_of = jnp.arange(width, dtype=jnp.int32) // c_in
    total = jnp.zeros((rows, width), jnp.float32)
    for k in range(KERNEL):
        total = total + jnp.where((tap_of == k)[None, :], product[4 - k : 4 - k + rows], 0.0)
    partial_input = total.reshape(rows, KERNEL, c_in).sum(axis=1)
    input_grad = lax.psum_scatter(partial_input, "section", scatter_dimension=1, tiled=True).astype(
        jnp.bfloat16
    )
    filter_grad = lax.psum_scatter(whole_term, "seq", scatter_dimension=0, tiled=True)
    return (input_grad, filter_grad)


def solution(mesh):
    in_specs = (P("seq", None), P("seq", "section"), P("seq", "section"), P("seq", "section"))
    out_specs = (P("seq", "section"), P("seq", "section"))
    return jax.shard_map(shards, mesh=mesh, in_specs=in_specs, out_specs=out_specs, check_vma=False)
```

profile of v0, /device:TPU:8, one launch (start us, length us, event | category | flops | bytes accessed | tf_op | source)
XLA Modules:
  0.0 342.2 jit_solution(12863627836406627910)
XLA Ops:
  7.2 0.0 copy-start
  7.2 0.0 all-gather.3.cloned.1.call-start
  7.2 0.7 all-gather.3.cloned.1.call-update
  7.9 0.0 all-reduce.3.cloned.1.call-start
  8.0 0.9 convert_multiply_fusion.4
  8.9 0.1 broadcast_in_dim.46
  9.0 0.3 mul.55
  9.3 1.1 fusion.16
  10.4 7.1 %collective-permute-start.1 = (bf16[2,384]{1,0:T(2,128)(2,1)S(1)}, bf16[2,384]{1,0:T(2,128)(2,1)S(1)}, u32[]{:S(2)}, u32[]{:S(2)}) collective-permute-start(bf16[2,384]{1,0:T(2,128)(2,1)S(1)} %get-tuple-element.9), channel_id=1, source_target_pairs={{4,0},{8,4},{12,8},{16,12},{20,16},{24,20},{28,24},{32,28},{36,32}... | collective-permute-start | bytes 4616 | tf_op jit(solution)/shard_map/ppermute | solution.py:19
  17.5 1.9 collective-permute-start
  19.5 0.0 collective-permute-done.1
  19.5 5.0 %collective-permute-done = bf16[2,384]{1,0:T(2,128)(2,1)S(1)} collective-permute-done((bf16[2,384]{1,0:T(2,128)(2,1)S(1)}, bf16[2,384]{1,0:T(2,128)(2,1)S(1)}, u32[]{:S(2)}, u32[]{:S(2)}) %collective-permute-start) | collective-permute-done | bytes 1568 | tf_op jit(solution)/shard_map/ppermute | solution.py:18
  24.5 0.1 maximum_multiply_fusion
  24.6 0.0 copy-done
  24.7 0.5 fusion.8
  25.2 0.5 fusion.7
  25.7 0.5 fusion.6
  26.2 0.5 fusion.5
  26.7 0.5 fusion.4
  27.2 4.6 %broadcast_multiply_fusion = f32[7040,384]{0,1:T(8,128)} fusion(f32[7040,384]{0,1:T(8,128)S(1)} %fusion.4), kind=kLoop, calls=%fused_computation.9 | loop fusion | flops 2703360 | bytes 21626880 | tf_op jit(solution)/shard_map/mul | solution.py:44
  31.8 0.0 all-reduce.3.cloned.1.call-update
  31.8 0.0 reduce-scatter.3.cloned.1.call-start
  32.0 60.9 %all-gather.3.cloned.1.call-done = bf16[64,110,384]{2,1,0:T(8,128)(2,1)} async-done(((bf16[1,110,384]{2,1,0:T(8,128)(2,1)}), bf16[64,110,384]{2,1,0:T(8,128)(2,1)}) %all-gather.3.cloned.1.call-update) | async-done | bytes 5406736 | tf_op jit(solution)/shard_map/all_gather | solution.py:58
  92.9 7.7 %reshape.59 = bf16[7040,384]{1,0:T(8,128)(2,1)} reshape(bf16[64,110,384]{2,1,0:T(8,128)(2,1)} %all-gather.3.cloned.1.call-done) | data formatting | bytes 10813440
  100.6 4.7 %fusion.30 = f32[260,7040]{1,0:T(8,128)S(1)} fusion(bf16[7040,384]{1,0:T(8,128)(2,1)} %reshape.59, bf16[2,384]{1,0:T(2,128)(2,1)S(1)} %collective-permute-done.1, bf16[256,384]{1,0:T(8,128)(2,1)S(1)} %fusion.16, bf16[2,384]{1,0:T(2,128)(2,1)S(1)} %collective-permute-done, bf16[260]{0:T(512)(128)(2,1)S(1)} %fusion.29), kind=kOutput, calls=%fused_computation.63 | convolution fusion | flops 1406545920 | bytes 12928520 | tf_op jit(solution)/shard_map/ro,no->rn/dot_general | solution.py:60
  105.3 6.0 %fusion = f32[256,7040]{1,0:T(8,128)} fusion(f32[260,7040]{1,0:T(8,128)S(1)} %fusion.30, pred[7040]{0:T(1024)(128)(4,1)S(1)} %get-tuple-element.10, pred[7040]{0:T(1024)(128)(4,1)S(1)} %get-tuple-element.11, pred[7040]{0:T(1024)(128)(4,1)S(1)} %get-tuple-element.12, pred[7040]{0:T(1024)(128)(4,1)S(1)} %broadcast_compare_fusion.4, ...), kind=kLoop, calls=%fused_computation.1 | loop fusion | flops 16220160 | bytes 43288960 | tf_op jit(solution)/shard_map/add | solution.py:64
  111.3 0.0 copy-start.1
  111.3 8.8 %copy.9 = f32[256,7040]{0,1:T(8,128)} copy(f32[256,7040]{1,0:T(8,128)} %fusion) | data formatting | bytes 14417920 | tf_op jit(solution)/shard_map/add | solution.py:64
  120.1 0.0 copy-start.2
  120.1 4.9 %reduce_sum.9 = f32[256,1408]{0,1:T(8,128)} reduce(f32[256,5,1408]{0,2,1:T(8,128)} %bitcast.31, f32[]{:T(128)} %constant.61.clone.1), dimensions={1}, to_apply=%region_0.1 | reduce | flops 1441792 | bytes 8650756 | tf_op jit(solution)/shard_map/reduce_sum | solution.py:65
  125.0 0.0 reduce-scatter.3.cloned.1.call-update
  125.1 0.0 copy-done.2
  125.1 0.6 dynamic-slice
  126.3 178.5 %all-reduce.3.cloned.1.call-done = f32[7040,384]{0,1:T(8,128)} async-done(((f32[7040,384]{0,1:T(8,128)}), f32[7040,384]{0,1:T(8,128)}) %all-reduce.3.cloned.1.call-update) | async-done | bytes 10813456
  304.9 1.1 constant_dynamic-slice_fusion
  306.0 0.8 copy.10
  306.8 27.2 %reduce-scatter.3.cloned.1.call-done = f32[256,352]{0,1:T(8,128)} async-done(((f32[256,1408]{0,1:T(8,128)}), f32[256,352]{0,1:T(8,128)}) %reduce-scatter.3.cloned.1.call-update) | async-done | bytes 360464 | tf_op jit(solution)/shard_map/reduce_scatter | solution.py:66
  334.0 1.7 convert_element_type.23
  335.7 0.0 copy-done.1
  (5 shorter events, 0.1 us)
Async XLA Ops:
  7.2 17.5 %copy-start = (bf16[256,1408]{1,0:T(8,128)(2,1)S(1)}, bf16[256,1408]{1,0:T(8,128)(2,1)}, u32[]{:S(2)}) copy-start(bf16[256,1408]{1,0:T(8,128)(2,1)} %param.4) | copy-start | bytes 2162692
  7.2 85.7 %all-gather.3.cloned.1.call-start = ((), (), s32[]{:S(2)}) async-start(), calls=%async_computation.2 | async-start | bytes 5591040 | tf_op jit(solution)/shard_map/all_gather | solution.py:58
  7.9 297.0 %all-reduce.3.cloned.1.call-start = ((), (), s32[]{:S(2)}) async-start(), calls=%async_computation.3 | async-start | bytes 21626880
  10.4 9.1 %collective-permute-start.1 = (bf16[2,384]{1,0:T(2,128)(2,1)S(1)}, bf16[2,384]{1,0:T(2,128)(2,1)S(1)}, u32[]{:S(2)}, u32[]{:S(2)}) collective-permute-start(bf16[2,384]{1,0:T(2,128)(2,1)S(1)} %get-tuple-element.9), channel_id=1, source_target_pairs={{4,0},{8,4},{12,8},{16,12},{20,16},{24,20},{28,24},{32,28},{36,32}... | collective-permute-start | bytes 4616 | tf_op jit(solution)/shard_map/ppermute | solution.py:19
  17.5 7.0 %collective-permute-start = (bf16[2,384]{1,0:T(2,128)(2,1)S(1)}, bf16[2,384]{1,0:T(2,128)(2,1)S(1)}, u32[]{:S(2)}, u32[]{:S(2)}) collective-permute-start(bf16[2,384]{1,0:T(2,128)(2,1)S(1)} %get-tuple-element.8), channel_id=1, source_target_pairs={{0,4},{4,8},{8,12},{12,16},{16,20},{20,24},{24,28},{28,32},{32,36}... | collective-permute-start | bytes 4616 | tf_op jit(solution)/shard_map/ppermute | solution.py:18
  31.8 302.2 %reduce-scatter.3.cloned.1.call-start = ((), (), s32[]{:S(2)}) async-start(), calls=%async_computation.1 | async-start | bytes 1802240 | tf_op jit(solution)/shard_map/reduce_scatter | solution.py:66
  111.3 224.4 %copy-start.1 = (bf16[256,1408]{1,0:T(8,128)(2,1)S(1)}, bf16[256,1408]{1,0:T(8,128)(2,1)}, u32[]{:S(2)}) copy-start(bf16[256,1408]{1,0:T(8,128)(2,1)} %param.4) | copy-start | bytes 2162692
  120.1 5.0 %copy-start.2 = (u32[256]{0:T(256)S(1)}, u32[256]{0:T(256)}, u32[]{:S(2)}) copy-start(u32[256]{0:T(256)} %constant.69) | copy-start | bytes 3076
Sparse Core Ops, SparseCore 0:
  10.7 82.1 all-gather.2
  96.5 208.2 all-reduce.2
  307.6 26.3 reduce-scatter.2
where the time goes:
time: 343 us; the launch traced here: 342 us
  waiting for transfers between devices  272 us (79%)
  local copies, waits for them, and re-layouts  19.5 us (6%)
  other arithmetic  19.4 us (6%)
  between operations  14.6 us (4%)
  starting transfers between devices  9.13 us (3%)
  matrix products  7.19 us (2%)
    unnamed x4, waiting for transfers between devices  179 us
    all_gather x1, waiting for transfers between devices, shards(): piece = lax.all_gather(filters, 'seq', axis=0, tiled=True)  60.9 us
    reduce_scatter x1, waiting for transfers between devices, shards(): lax.psum_scatter(partial_input, 'section', scatter_dimension=1, tiled=True)  27.2 us
    unnamed x10, local copies, waits for them, and re-layouts  10.3 us
    add x1, local copies, waits for them, and re-layouts, shards(): total + jnp.where((tap_of == k)[None, :], product[4 - k:4 - k + rows], 0.0)  8.77 us
    ppermute x1, starting transfers between devices, with_halo(): after = lax.ppermute(first, axis, down)  7.09 us
  transfers between devices with their start and end apart: 5, of which 4 were waited for; matrix products, arithmetic and copies ran while one was open for 13% of the time, Pallas kernels for 0%

commit v1 on v0

--- a/solution.py
+++ b/solution.py
@@ -55,7 +55,11 @@
         )
         * scale_value
     )
-    piece = lax.all_gather(filters, "seq", axis=0, tiled=True)
+    length_2 = lax.axis_size("seq")
+    repeats = [length_2 if d == 0 else 1 for d in range(filters.ndim)]
+    piece = lax.all_to_all(
+        jnp.tile(filters, repeats), "seq", split_axis=0, concat_axis=0, tiled=True
+    )
     width = piece.shape[0]
     product = jnp.einsum("ro,no->rn", grad_rim, piece, preferred_element_type=jnp.float32)
     tap_of = jnp.arange(width, dtype=jnp.int32) // c_in

time: 343 us -> 374 us (1.090)
  waiting for transfers between devices: 272 us -> 290 us
  starting transfers between devices: 9.13 us -> 18.7 us
  local copies, waits for them, and re-layouts: 19.5 us -> 23.4 us
    ppermute x1, waiting for transfers between devices: 0.01 us -> 109 us  [with_halo(): after = lax.ppermute(first, axis, down)]
    all_gather x1 -> x0, waiting for transfers between devices: 60.9 us -> none  [shards(): piece = lax.all_gather(filters, 'seq', axis=0, tiled=True)]
    reduce_scatter x1, waiting for transfers between devices: 27.2 us -> 0.01 us  [shards(): lax.psum_scatter(partial_input, 'section', scatter_dimension=1, tiled=True)]
    all_to_all x0 -> x1, starting transfers between devices: none -> 12.4 us  [shards(): lax.all_to_all(jnp.tile(filters, repeats), 'seq', split_axis=0, concat_ax...]
    all_to_all x0 -> x1, local copies, waits for them, and re-layouts: none -> 7.77 us  [shards(): lax.all_to_all(jnp.tile(filters, repeats), 'seq', split_axis=0, concat_ax...]
    unnamed x10 -> x13, local copies, waits for them, and re-layouts: 10.3 us -> 2.53 us
    another operation x0 -> x1, local copies, waits for them, and re-layouts: none -> 3.9 us  [shards(): jnp.tile(filters, repeats)]
    unnamed x4 -> x3, waiting for transfers between devices: 179 us -> 179 us
  transfers between devices with their start and end apart: 5 -> 5, of which waited for: 4 -> 3; matrix products, arithmetic and copies ran while one was open for 13% -> 9% of each run, Pallas kernels for 0% -> 0%
where the time goes in v1:
time: 374 us; the launch traced here: 373 us
  waiting for transfers between devices  290 us (78%)
  local copies, waits for them, and re-layouts  23.4 us (6%)
  starting transfers between devices  18.7 us (5%)
  other arithmetic  17.6 us (5%)
  between operations  16.3 us (4%)
  matrix products  7.19 us (2%)
    unnamed x3, waiting for transfers between devices  179 us
    ppermute x1, waiting for transfers between devices, with_halo(): after = lax.ppermute(first, axis, down)  109 us
    all_to_all x1, starting transfers between devices, shards(): lax.all_to_all(jnp.tile(filters, repeats), 'seq', split_axis=0, concat_ax...  12.4 us
    add x1, local copies, waits for them, and re-layouts, shards(): total + jnp.where((tap_of == k)[None, :], product[4 - k:4 - k + rows], 0.0)  8.76 us
    all_to_all x1, local copies, waits for them, and re-layouts, shards(): lax.all_to_all(jnp.tile(filters, repeats), 'seq', split_axis=0, concat_ax...  7.77 us
  transfers between devices with their start and end apart: 5, of which 3 were waited for; matrix products, arithmetic and copies ran while one was open for 9% of the time, Pallas kernels for 0%

profile of v1, /device:TPU:8, one launch (start us, length us, event | category | flops | bytes accessed | tf_op | source)
XLA Modules:
  0.0 373.3 jit_solution(4896163097983277382)
XLA Ops:
  8.0 0.0 copy-start
  8.0 0.0 copy-start.3
  8.0 3.9 %tile.2 = bf16[64,110,384]{2,1,0:T(8,128)(2,1)} broadcast(bf16[110,384]{1,0:T(8,128)(2,1)} %param.7), dimensions={1,2} | broadcast | bytes 5491200 | tf_op jit(solution)/shard_map/tile | solution.py:61
  11.9 0.0 copy-start.2
  11.9 12.4 %all-to-all-start = ((bf16[64,110,384]{2,1,0:T(8,128)(2,1)}), bf16[64,110,384]{2,1,0:T(8,128)(2,1)}, u32[]{:S(2)}, u32[]{:S(2)}) async-start(bf16[64,110,384]{2,1,0:T(8,128)(2,1)} %tile.2), calls=%async_computation | async-start | bytes 11010048 | tf_op jit(solution)/shard_map/all_to_all | solution.py:60
  24.3 0.0 all-reduce.3.cloned.1.call-start
  24.4 0.0 copy-done.3
  24.4 0.1 broadcast_in_dim.46
  24.6 0.3 mul.55
  24.9 0.0 copy-done.2
  24.9 0.2 fusion.16
  25.1 4.3 %collective-permute-start.1 = (bf16[2,384]{1,0:T(2,128)(2,1)S(1)}, bf16[2,384]{1,0:T(2,128)(2,1)S(1)}, u32[]{:S(2)}, u32[]{:S(2)}) collective-permute-start(bf16[2,384]{1,0:T(2,128)(2,1)S(1)} %get-tuple-element.9), channel_id=1, source_target_pairs={{4,0},{8,4},{12,8},{16,12},{20,16},{24,20},{28,24},{32,28},{36,32}... | collective-permute-start | bytes 4616 | tf_op jit(solution)/shard_map/ppermute | solution.py:19
  29.4 1.9 collective-permute-start
  31.4 109.3 %collective-permute-done.1 = bf16[2,384]{1,0:T(2,128)(2,1)S(1)} collective-permute-done((bf16[2,384]{1,0:T(2,128)(2,1)S(1)}, bf16[2,384]{1,0:T(2,128)(2,1)S(1)}, u32[]{:S(2)}, u32[]{:S(2)}) %collective-permute-start.1) | collective-permute-done | bytes 1568 | tf_op jit(solution)/shard_map/ppermute | solution.py:19
  140.7 2.0 collective-permute-done
  142.7 0.1 maximum_multiply_fusion
  142.8 0.0 copy-done
  142.8 0.5 fusion.8
  143.3 0.5 fusion.7
  143.8 0.5 fusion.6
  144.3 0.5 fusion.5
  144.8 0.5 fusion.4
  145.3 4.6 %broadcast_multiply_fusion = f32[7040,384]{0,1:T(8,128)} fusion(f32[7040,384]{0,1:T(8,128)S(1)} %fusion.4), kind=kLoop, calls=%fused_computation.9 | loop fusion | flops 2703360 | bytes 21626880 | tf_op jit(solution)/shard_map/mul | solution.py:44
  149.9 0.0 all-reduce.3.cloned.1.call-update
  150.0 0.0 reduce-scatter.3.cloned.1.call-start
  150.1 0.0 all-to-all-done
  150.1 7.8 %all_to_all.7 = bf16[7040,384]{1,0:T(8,128)(2,1)} reshape(bf16[64,110,384]{2,1,0:T(8,128)(2,1)} %all-to-all-done) | data formatting | bytes 10813440 | tf_op jit(solution)/shard_map/all_to_all | solution.py:60
  157.9 4.7 %fusion.30 = f32[260,7040]{1,0:T(8,128)S(1)} fusion(bf16[7040,384]{1,0:T(8,128)(2,1)} %all_to_all.7, bf16[2,384]{1,0:T(2,128)(2,1)S(1)} %collective-permute-done.1, bf16[256,384]{1,0:T(8,128)(2,1)S(1)} %fusion.16, bf16[2,384]{1,0:T(2,128)(2,1)S(1)} %collective-permute-done, bf16[260]{0:T(512)(128)(2,1)S(1)} %fusion.29), kind=kOutput, calls=%fused_computation.63 | convolution fusion | flops 1406545920 | bytes 12928520 | tf_op jit(solution)/shard_map/ro,no->rn/dot_general | solution.py:64
  162.6 6.0 %fusion = f32[256,7040]{1,0:T(8,128)} fusion(f32[260,7040]{1,0:T(8,128)S(1)} %fusion.30, pred[7040]{0:T(1024)(128)(4,1)S(1)} %get-tuple-element.10, pred[7040]{0:T(1024)(128)(4,1)S(1)} %get-tuple-element.11, pred[7040]{0:T(1024)(128)(4,1)S(1)} %get-tuple-element.12, pred[7040]{0:T(1024)(128)(4,1)S(1)} %broadcast_compare_fusion.4, ...), kind=kLoop, calls=%fused_computation.1 | loop fusion | flops 16220160 | bytes 43288960 | tf_op jit(solution)/shard_map/add | solution.py:68
  168.6 0.0 copy-start.1
  168.6 8.8 %copy.9 = f32[256,7040]{0,1:T(8,128)} copy(f32[256,7040]{1,0:T(8,128)} %fusion) | data formatting | bytes 14417920 | tf_op jit(solution)/shard_map/add | solution.py:68
  177.3 0.0 copy-start.4
  177.3 4.9 %reduce_sum.9 = f32[256,1408]{0,1:T(8,128)} reduce(f32[256,5,1408]{0,2,1:T(8,128)} %bitcast.30, f32[]{:T(128)} %constant.61.clone.1), dimensions={1}, to_apply=%region_0.1 | reduce | flops 1441792 | bytes 8650756 | tf_op jit(solution)/shard_map/reduce_sum | solution.py:69
  182.3 0.0 reduce-scatter.3.cloned.1.call-update
  182.3 0.0 copy-done.4
  182.3 0.6 dynamic-slice
  183.5 178.7 %all-reduce.3.cloned.1.call-done = f32[7040,384]{0,1:T(8,128)} async-done(((f32[7040,384]{0,1:T(8,128)}), f32[7040,384]{0,1:T(8,128)}) %all-reduce.3.cloned.1.call-update) | async-done | bytes 10813456
  362.3 1.1 constant_dynamic-slice_fusion
  363.4 0.8 copy.10
  364.2 0.0 reduce-scatter.3.cloned.1.call-done
  364.2 1.7 convert_element_type.23
  365.9 0.0 copy-done.1
  (6 shorter events, 0.1 us)
Async XLA Ops:
  8.0 134.8 %copy-start = (bf16[256,1408]{1,0:T(8,128)(2,1)S(1)}, bf16[256,1408]{1,0:T(8,128)(2,1)}, u32[]{:S(2)}) copy-start(bf16[256,1408]{1,0:T(8,128)(2,1)} %param.4) | copy-start | bytes 2162692
  8.0 16.4 %copy-start.3 = (bf16[128,384]{1,0:T(8,128)(2,1)S(1)}, bf16[128,384]{1,0:T(8,128)(2,1)}, u32[]{:S(2)}) copy-start(bf16[128,384]{1,0:T(8,128)(2,1)} %param.6) | copy-start | bytes 294916
  11.9 12.9 %copy-start.2 = (bf16[256,384]{1,0:T(8,128)(2,1)S(1)}, bf16[256,384]{1,0:T(8,128)(2,1)}, u32[]{:S(2)}) copy-start(bf16[256,384]{1,0:T(8,128)(2,1)} %param.5) | copy-start | bytes 589828
  11.9 138.2 %all-to-all-start = ((bf16[64,110,384]{2,1,0:T(8,128)(2,1)}), bf16[64,110,384]{2,1,0:T(8,128)(2,1)}, u32[]{:S(2)}, u32[]{:S(2)}) async-start(bf16[64,110,384]{2,1,0:T(8,128)(2,1)} %tile.2), calls=%async_computation | async-start | bytes 11010048 | tf_op jit(solution)/shard_map/all_to_all | solution.py:60
  24.3 337.9 %all-reduce.3.cloned.1.call-start = ((), (), s32[]{:S(2)}) async-start(), calls=%async_computation.3 | async-start | bytes 21626880
  25.1 115.6 %collective-permute-start.1 = (bf16[2,384]{1,0:T(2,128)(2,1)S(1)}, bf16[2,384]{1,0:T(2,128)(2,1)S(1)}, u32[]{:S(2)}, u32[]{:S(2)}) collective-permute-start(bf16[2,384]{1,0:T(2,128)(2,1)S(1)} %get-tuple-element.9), channel_id=1, source_target_pairs={{4,0},{8,4},{12,8},{16,12},{20,16},{24,20},{28,24},{32,28},{36,32}... | collective-permute-start | bytes 4616 | tf_op jit(solution)/shard_map/ppermute | solution.py:19
  29.4 113.3 %collective-permute-start = (bf16[2,384]{1,0:T(2,128)(2,1)S(1)}, bf16[2,384]{1,0:T(2,128)(2,1)S(1)}, u32[]{:S(2)}, u32[]{:S(2)}) collective-permute-start(bf16[2,384]{1,0:T(2,128)(2,1)S(1)} %get-tuple-element.8), channel_id=1, source_target_pairs={{0,4},{4,8},{8,12},{12,16},{16,20},{20,24},{24,28},{28,32},{32,36}... | collective-permute-start | bytes 4616 | tf_op jit(solution)/shard_map/ppermute | solution.py:18
  150.0 214.3 %reduce-scatter.3.cloned.1.call-start = ((), (), s32[]{:S(2)}) async-start(), calls=%async_computation.2 | async-start | bytes 1802240 | tf_op jit(solution)/shard_map/reduce_scatter | solution.py:70
  168.6 197.3 %copy-start.1 = (bf16[256,1408]{1,0:T(8,128)(2,1)S(1)}, bf16[256,1408]{1,0:T(8,128)(2,1)}, u32[]{:S(2)}) copy-start(bf16[256,1408]{1,0:T(8,128)(2,1)} %param.4) | copy-start | bytes 2162692
  177.3 5.0 %copy-start.4 = (u32[256]{0:T(256)S(1)}, u32[256]{0:T(256)}, u32[]{:S(2)}) copy-start(u32[256]{0:T(256)} %constant.69) | copy-start | bytes 3076
Sparse Core Ops, SparseCore 0:
  150.1 212.1 all-reduce.2
Sparse Core Ops, SparseCore 1:
  182.4 29.2 reduce-scatter.2
